TPU v7x, 32 devices: a whole 2x2x4 slice. The times are simulated.
32 devices in a mesh: grp: 4 (over z), mem: 8 (over y, x, core).
Axes of the slice: x: 2, y: 2, z: 4, core: 2. Of those that a mesh axis runs over, the one named last changes fastest.
Arguments:
- volume: float32 [4, 8, 8, 512, 1024], P('grp', 'mem'), may hold values from -1 to 1
- transfer_coef: float32 [4, 4], replicated, may hold values from -3 to 3
- group_order: int32 [4], replicated, may hold values from 0 to 3, each once
- member_order: int32 [4, 8], replicated, may hold values from 0 to 7, each once within a row
- active_mask: int32 [4, 8], P('grp', 'mem'), may hold values 0 or 1
Outputs:
- picture: float32 [4, 512, 1024], P(None, 'mem', 'grp')
All inputs are finite; a program needn't handle non-finite values. No bound on the sum of `active_mask` on one device may be relied on, other than what follows from the above.
Results may differ from a plain program's by a relative error of at most 0.0003.
Values sent between devices are 32-bit elements; how exact they have to be, the bound alone decides.
A program may use at most 192 MiB of HBM per device.

v0:
```python
import jax
import jax.numpy as jnp
from jax import lax
from jax.sharding import PartitionSpec as P


def polynomial(coef_row, values):
    return coef_row[0] + values * (coef_row[1] + values * (coef_row[2] + values * coef_row[3]))


def march_brick(samples, transfer_coef, active_flag, density_scale):
    optical_depth = jnp.zeros(samples.shape[1:], jnp.float32)
    colour = jnp.zeros((3,) + samples.shape[1:], jnp.float32)
    for sample_index in range(samples.shape[0]):
        values = samples[sample_index]
        extinction = polynomial(transfer_coef[3], values) ** 2 * density_scale
        opacity = 1.0 - jnp.exp(-extinction)
        tinted = jax.nn.sigmoid(
            jnp.stack([polynomial(transfer_coef[channel], values) for channel in range(3)])
        )
        colour = colour + (jnp.exp(-optical_depth) * opacity)[None] * tinted
        optical_depth = optical_depth + extinction
    coverage = 1.0 - jnp.exp(-optical_depth)
    return jnp.concatenate([colour, coverage[None]], 0) * active_flag


def reorder(layers, rank_list):
    total = rank_list.shape[0]
    positions = jnp.arange(total, dtype=jnp.int32)
    inverse = jnp.sum(
        positions[:, None] * (rank_list[:, None] == positions[None, :]).astype(jnp.int32), axis=0
    )
    return jnp.take(layers, inverse, axis=0)


def over_tree(layers):
    while layers.shape[0] > 1:
        nearer = layers[0::2]
        farther = layers[1::2]
        layers = nearer + (1.0 - nearer[:, 3:4]) * farther
    return layers[0]


def body(volume, transfer_coef, group_order, member_order, active_mask):
    groups = lax.axis_size("grp")
    members = lax.axis_size("mem")
    density_scale = 3.0 / (volume.shape[2] * groups * members)
    active_flag = active_mask[0, 0].astype(jnp.float32)
    layer = march_brick(volume[0, 0], transfer_coef, active_flag, density_scale)
    slab_ranks = lax.dynamic_slice_in_dim(member_order, lax.axis_index("grp"), 1, 0)[0]
    slab_image = over_tree(
        reorder(
            lax.all_to_all(layer[None], "mem", split_axis=2, concat_axis=0, tiled=True), slab_ranks
        )
    )
    return over_tree(
        reorder(
            lax.all_to_all(slab_image[None], "grp", split_axis=3, concat_axis=0, tiled=True),
            group_order,
        )
    )


def solution(mesh):
    in_specs = (P("grp", "mem", None, None, None), P(), P(), P(), P("grp", "mem"))
    out_specs = P(None, "mem", "grp")
    return jax.shard_map(body, mesh=mesh, in_specs=in_specs, out_specs=out_specs, check_vma=False)
```

profile of v0, /device:TPU:2, one launch (start us, length us, event | category | flops | bytes accessed | tf_op | source)
XLA Modules:
  0.0 448.7 jit_solution(17760567947958751179)
XLA Ops:
  0.0 6.7 %slice_bitcast_fusion = (f32[1,512,1024]{2,1,0:T(8,128)S(1)}, f32[1,1,1,512,1024]{4,3,2,1,0:T(8,128)S(1)}, f32[1,1,1,512,1024]{4,3,2,1,0:T(8,128)S(1)}, f32[1,1,...) fusion(f32[1,1,8,512,1024]{4,3,2,1,0:T(8,128)} %param.5), kind=kLoop, calls=%fused_computation.159 | loop fusion | bytes 33554432 | tf_op jit(solution)/shard_map/squeeze | solution.py:15
  6.7 0.9 fusion.105
  7.6 31.3 %multiply_add_fusion.4 = (f32[1,512,1024]{2,0,1:T(1,128)}, f32[1,512,1024]{2,0,1:T(1,128)}, f32[1,512,1024]{2,0,1:T(1,128)}, f32[1,512,1024]{2,0,1:T(1,128)}, f3...) fusion(f32[]{:T(128)} %bitcast.9, f32[]{:T(128)} %bitcast.8, f32[]{:T(128)} %bitcast.7, f32[]{:T(128)} %bitcast.6, ...), kind=kLoop, calls=%fused_computation.130 | loop fusion | flops 18874368 | bytes 16777264 | tf_op jit(solution)/shard_map/add | solution.py:8
  39.0 30.7 %multiply_add_fusion.10 = (f32[1,512,1024]{2,0,1:T(1,128)}, f32[1,512,1024]{2,0,1:T(1,128)}, f32[1,512,1024]{2,0,1:T(1,128)}, f32[1,512,1024]{2,0,1:T(1,128)}, f...) fusion(f32[1,1,1,512,1024]{4,3,2,1,0:T(8,128)S(1)} %get-tuple-element.16, f32[]{:T(128)} %bitcast.9, f32[]{:T(128)} %bitcast.8, ...), kind=kLoop, calls=%fused_computation.137 | loop fusion | flops 18874368 | bytes 16777264 | tf_op jit(solution)/shard_map/add | solution.py:8
  69.6 30.7 %multiply_add_fusion.16 = (f32[1,512,1024]{2,0,1:T(1,128)}, f32[1,512,1024]{2,0,1:T(1,128)}, f32[1,512,1024]{2,0,1:T(1,128)}, f32[1,512,1024]{2,0,1:T(1,128)}, f...) fusion(f32[1,1,1,512,1024]{4,3,2,1,0:T(8,128)S(1)} %get-tuple-element.18, f32[]{:T(128)} %bitcast.9, f32[]{:T(128)} %bitcast.8, ...), kind=kLoop, calls=%fused_computation.145 | loop fusion | flops 18874368 | bytes 16777264 | tf_op jit(solution)/shard_map/add | solution.py:8
  100.3 32.0 %multiply_add_fusion.22 = (f32[1,512,1024]{2,0,1:T(1,128)}, f32[1,512,1024]{2,0,1:T(1,128)}, f32[1,512,1024]{2,0,1:T(1,128)}, f32[1,512,1024]{2,0,1:T(1,128)}, f...) fusion(f32[1,1,1,512,1024]{4,3,2,1,0:T(8,128)S(1)} %get-tuple-element.20, f32[]{:T(128)} %bitcast.9, f32[]{:T(128)} %bitcast.8, ...), kind=kLoop, calls=%fused_computation.153 | loop fusion | flops 18874368 | bytes 16777264 | tf_op jit(solution)/shard_map/add | solution.py:8
  132.3 41.6 %fusion.86 = f32[1,1,512,1024]{3,1,0,2:T(1,128)} fusion(f32[1,1,1,512,1024]{4,3,2,1,0:T(8,128)S(1)} %get-tuple-element.16, f32[1,1,1,512,1024]{4,3,2,1,0:T(8,128)S(1)} %get-tuple-element.17, f32[1,1,1,512,1024]{4,3,2,1,0:T(8,128)S(1)} %get-tuple-element.18, f32[1,1,1,512,1024]{4,3,2,1,0:T(8,128)S(1)} %get-tuple-element.19, ...), kind=kLoop, calls=%fused_computation.126 | loop fusion | flops 34603008 | bytes 18874384 | tf_op jit(solution)/shard_map/concatenate | solution.py:24
  174.0 6.2 %subtract_multiply_fusion.3 = (f32[512,1024]{1,0:T(8,128)}, f32[512,1024]{1,0:T(8,128)S(1)}) fusion(f32[]{:T(128)} %bitcast.5, f32[]{:T(128)} %bitcast.4, f32[]{:T(128)} %bitcast.3, f32[]{:T(128)} %bitcast.1, f32[1,1,8,512,1024]{4,3,2,1,0:T(8,128)S(1)} %bitcast.282), kind=kLoop, calls=%fused_computation.146 | loop fusion | flops 19922944 | bytes 12582928 | tf_op jit(solution)/shard_map/mul | solution.py:21
  180.2 6.7 %subtract_multiply_fusion.1 = (f32[512,1024]{1,0:T(8,128)}, f32[512,1024]{1,0:T(8,128)S(1)}, f32[512,1024]{1,0:T(8,128)}) fusion(f32[]{:T(128)} %bitcast.5, f32[]{:T(128)} %bitcast.4, f32[]{:T(128)} %bitcast.3, f32[]{:T(128)} %bitcast.1, f32[1,1,8,512,1024]{4,3,2,1,0:T(8,128)S(1)} %bitcast.282, f32[512,1024]{1,0:T(8,128)S(1)} %get-tuple-element.6), kind=kLoop, calls=%fused_computation.138 | loop fusion | flops 17825792 | bytes 14680080 | tf_op jit(solution)/shard_map/mul | solution.py:21
  187.0 11.5 %subtract_multiply_fusion = (f32[512,1024]{1,0:T(8,128)}, f32[512,1024]{1,0:T(8,128)}, f32[512,1024]{1,0:T(8,128)}, f32[512,1024]{1,0:T(8,128)}, f32[512,1024]{1,0:T(8,128)}) fusion(f32[]{:T(128)} %bitcast.5, f32[]{:T(128)} %bitcast.4, f32[]{:T(128)} %bitcast.3, f32[]{:T(128)} %bitcast.1, f32[512,1024]{1,0:T(8,128)S(1)} %get-tuple-element.8, ...), kind=kLoop, calls=%fused_computation.134 | loop fusion | flops 35651584 | bytes 25165840 | tf_op jit(solution)/shard_map/mul | solution.py:21
  199.2 75.1 %fusion.39 = f32[1,3,512,1024]{3,1,0,2:T(4,128)S(1)} fusion(f32[1,512,1024]{2,0,1:T(1,128)S(1)} %copy-done.4, f32[1,512,1024]{2,0,1:T(1,128)S(1)} %copy-done.5, f32[1,512,1024]{2,0,1:T(1,128)S(1)} %copy-done.3, f32[1,512,1024]{2,0,1:T(1,128)S(1)} %copy-done.6, f32[1,512,1024]{2,0,1:T(1,128)S(1)} %copy-done.7, f32[1,512,1024]{2,0,1:T(1,128)S(1)} %copy-done.8, ...), kind=kLoop, calls=%fused_computation.51 | loop fusion | flops 86507520 | bytes 73400320 | tf_op jit(solution)/shard_map/concatenate | solution.py:24
  274.3 7.1 %maximum_multiply_fusion = f32[1,4,512,1024]{3,1,0,2:T(4,128)} fusion(f32[1,1,512,1024]{3,1,0,2:T(1,128)} %fusion.86, f32[1,3,512,1024]{3,1,0,2:T(4,128)S(1)} %fusion.39, f32[]{:T(128)} %bitcast.29), kind=kLoop, calls=%fused_computation.49 | loop fusion | flops 4194304 | bytes 16777220 | tf_op jit(solution)/shard_map/mul | solution.py:24
  281.4 5.1 %all-to-all-start = ((f32[1,4,512,1024]{3,1,0,2:T(4,128)}), f32[1,4,512,1024]{3,1,0,2:T(4,128)}, u32[]{:S(2)}, u32[]{:S(2)}) async-start(f32[1,4,512,1024]{3,1,0,2:T(4,128)} %maximum_multiply_fusion), calls=%async_computation | async-start | bytes 16777216 | tf_op jit(solution)/shard_map/all_to_all | solution.py:53
  286.6 92.2 %all-to-all-done = f32[1,4,512,1024]{3,1,0,2:T(4,128)} async-done(((f32[1,4,512,1024]{3,1,0,2:T(4,128)}), f32[1,4,512,1024]{3,1,0,2:T(4,128)}, u32[]{:S(2)}, u32[]{:S(2)}) %all-to-all-start) | async-done | bytes 8388640 | tf_op jit(solution)/shard_map/all_to_all | solution.py:53
  378.8 11.3 %copy.99 = f32[1,4,8,64,1024]{4,3,1,2,0:T(8,128)} copy(f32[1,4,8,64,1024]{4,1,3,2,0:T(4,128)} %bitcast.30) | data formatting | bytes 16777216 | tf_op jit(solution)/shard_map/all_to_all | solution.py:53
  390.1 7.7 %gather_fusion = f32[8,4,64,1024]{3,2,1,0:T(8,128)} fusion(f32[8,4,64,1024]{3,2,1,0:T(8,128)} %bitcast.283, s32[1024]{0:T(1024)S(1)} %pad_clamp_fusion.1), kind=kCustom, calls=%fused_computation | custom fusion | bytes 16777248 | tf_op jit(solution)/shard_map/jit(_take)/gather | solution.py:33
  397.9 4.4 broadcast_select_fusion
  402.3 0.5 slice.148
  402.9 1.1 multiply_add_fusion
  404.3 0.7 multiply_add_fusion.1
  405.0 0.2 fusion.93
  405.2 0.9 copy.75
  406.1 2.9 reshape.2041
  409.0 5.4 %all-to-all-start.1 = ((f32[4,1,65536]{2,1,0:T(1,128)}), f32[4,1,65536]{2,1,0:T(1,128)S(1)}, u32[]{:S(2)}, u32[]{:S(2)}) async-start(f32[4,1,65536]{2,1,0:T(1,128)} %reshape.2041), calls=%async_computation.1 | async-start | bytes 2097152 | tf_op jit(solution)/shard_map/all_to_all | solution.py:58
  414.6 25.8 %all-to-all-done.1 = f32[4,1,65536]{2,1,0:T(1,128)S(1)} async-done(((f32[4,1,65536]{2,1,0:T(1,128)}), f32[4,1,65536]{2,1,0:T(1,128)S(1)}, u32[]{:S(2)}, u32[]{:S(2)}) %all-to-all-start.1) | async-done | bytes 1048608 | tf_op jit(solution)/shard_map/all_to_all | solution.py:58
  440.4 0.5 broadcast.2075
  441.0 3.8 reduce
  444.7 1.4 reshape.2042
  446.2 0.8 copy.77
  447.0 0.6 gather_fusion.1
  447.6 0.2 broadcast_select_fusion.1
  448.0 0.7 fusion.97
  (48 shorter events, 0.7 us)
Async XLA Ops:
  0.0 286.5 %copy-start = (s32[4,8]{1,0:T(4,128)S(1)}, s32[4,8]{1,0:T(4,128)}, u32[]{:S(2)}) copy-start(s32[4,8]{1,0:T(4,128)} %param.8) | copy-start | bytes 388
  0.0 6.7 %copy-start.9 = (f32[4,4]{1,0:T(4,128)S(1)}, f32[4,4]{1,0:T(4,128)}, u32[]{:S(2)}) copy-start(f32[4,4]{1,0:T(4,128)} %param.6) | copy-start | bytes 196
  6.7 32.2 %copy-start.1 = (f32[1,1,1,512,1024]{4,3,2,1,0:T(8,128)}, f32[1,1,1,512,1024]{4,3,2,1,0:T(8,128)S(1)}, u32[]{:S(2)}) copy-start(f32[1,1,1,512,1024]{4,3,2,1,0:T(8,128)S(1)} %get-tuple-element.22) | copy-start | bytes 6291460
  100.3 32.0 %copy-start.2 = (f32[1,1,1,512,1024]{4,3,2,1,0:T(8,128)S(1)}, f32[1,1,1,512,1024]{4,3,2,1,0:T(8,128)}, u32[]{:S(2)}) copy-start(f32[1,1,1,512,1024]{4,3,2,1,0:T(8,128)} %copy-done.1) | copy-start | bytes 6291460
  100.3 73.6 %slice-start = ((s8[16777216]{0:T(1024)(128)(4,1)}), s8[4194304]{0:T(1024)(128)(4,1)S(1)}, s32[]{:S(2)}) async-start(s8[16777216]{0:T(1024)(128)(4,1)} %bitcast.281), calls=%async_computation.2 | async-start | bytes 8388608
  100.3 73.6 %slice-start.1 = ((s8[16777216]{0:T(1024)(128)(4,1)}), s8[4194304]{0:T(1024)(128)(4,1)S(1)}, s32[]{:S(2)}) async-start(s8[16777216]{0:T(1024)(128)(4,1)} %bitcast.281), calls=%async_computation.3 | async-start | bytes 8388608
  132.3 41.6 %slice-start.2 = ((s8[16777216]{0:T(1024)(128)(4,1)}), s8[4194304]{0:T(1024)(128)(4,1)S(1)}, s32[]{:S(2)}) async-start(s8[16777216]{0:T(1024)(128)(4,1)} %bitcast.281), calls=%async_computation.4 | async-start | bytes 8388608
  132.3 41.6 %slice-start.3 = ((s8[16777216]{0:T(1024)(128)(4,1)}), s8[4194304]{0:T(1024)(128)(4,1)S(1)}, s32[]{:S(2)}) async-start(s8[16777216]{0:T(1024)(128)(4,1)} %bitcast.281), calls=%async_computation.5 | async-start | bytes 8388608
  187.0 12.2 %copy-start.3 = (f32[1,512,1024]{2,0,1:T(1,128)S(1)}, f32[1,512,1024]{2,0,1:T(1,128)}, u32[]{:S(2)}) copy-start(f32[1,512,1024]{2,0,1:T(1,128)} %get-tuple-element.44) | copy-start | bytes 6291460
  187.0 12.2 %copy-start.4 = (f32[1,512,1024]{2,0,1:T(1,128)S(1)}, f32[1,512,1024]{2,0,1:T(1,128)}, u32[]{:S(2)}) copy-start(f32[1,512,1024]{2,0,1:T(1,128)} %get-tuple-element.45) | copy-start | bytes 6291460
  187.0 12.2 %copy-start.5 = (f32[1,512,1024]{2,0,1:T(1,128)S(1)}, f32[1,512,1024]{2,0,1:T(1,128)}, u32[]{:S(2)}) copy-start(f32[1,512,1024]{2,0,1:T(1,128)} %get-tuple-element.46) | copy-start | bytes 6291460
  187.0 12.2 %copy-start.6 = (f32[1,512,1024]{2,0,1:T(1,128)S(1)}, f32[1,512,1024]{2,0,1:T(1,128)}, u32[]{:S(2)}) copy-start(f32[1,512,1024]{2,0,1:T(1,128)} %get-tuple-element.63) | copy-start | bytes 6291460
  187.0 12.2 %copy-start.7 = (f32[1,512,1024]{2,0,1:T(1,128)S(1)}, f32[1,512,1024]{2,0,1:T(1,128)}, u32[]{:S(2)}) copy-start(f32[1,512,1024]{2,0,1:T(1,128)} %get-tuple-element.64) | copy-start | bytes 6291460
  187.0 12.2 %copy-start.8 = (f32[1,512,1024]{2,0,1:T(1,128)S(1)}, f32[1,512,1024]{2,0,1:T(1,128)}, u32[]{:S(2)}) copy-start(f32[1,512,1024]{2,0,1:T(1,128)} %get-tuple-element.65) | copy-start | bytes 6291460
  281.4 97.5 %all-to-all-start = ((f32[1,4,512,1024]{3,1,0,2:T(4,128)}), f32[1,4,512,1024]{3,1,0,2:T(4,128)}, u32[]{:S(2)}, u32[]{:S(2)}) async-start(f32[1,4,512,1024]{3,1,0,2:T(4,128)} %maximum_multiply_fusion), calls=%async_computation | async-start | bytes 16777216 | tf_op jit(solution)/shard_map/all_to_all | solution.py:53
  406.1 8.4 %copy-start.10 = (s32[4]{0:T(128)S(1)}, s32[4]{0:T(128)}, u32[]{:S(2)}) copy-start(s32[4]{0:T(128)} %param.7) | copy-start | bytes 52
  409.0 31.4 %all-to-all-start.1 = ((f32[4,1,65536]{2,1,0:T(1,128)}), f32[4,1,65536]{2,1,0:T(1,128)S(1)}, u32[]{:S(2)}, u32[]{:S(2)}) async-start(f32[4,1,65536]{2,1,0:T(1,128)} %reshape.2041), calls=%async_computation.1 | async-start | bytes 2097152 | tf_op jit(solution)/shard_map/all_to_all | solution.py:58
where the time goes:
time: 450 us; the launch traced here: 449 us
  other arithmetic  285 us (63%)
  waiting for transfers between devices  118 us (26%)
  local copies, waits for them, and re-layouts  34.6 us (8%)
  starting transfers between devices  10.6 us (2%)
    add x4, other arithmetic, polynomial(): coef_row[0]  125 us
    concatenate x2, other arithmetic, march_brick(): return jnp.concatenate([colour, coverage[None]], 0) * active_flag  117 us
    all_to_all x1, waiting for transfers between devices, body(): lax.all_to_all(layer[None], 'mem', split_axis=2, concat_axis=0, tiled=True)  92.2 us
    all_to_all x1, waiting for transfers between devices, body(): lax.all_to_all(slab_image[None], 'grp', split_axis=3, concat_axis=0, tile...  25.8 us
    mul x3, other arithmetic, march_brick(): colour = colour + (jnp.exp(-optical_depth) * opacity)[None] * tinted  24.5 us
    all_to_all x1, local copies, waits for them, and re-layouts, body(): lax.all_to_all(layer[None], 'mem', split_axis=2, concat_axis=0, tiled=True)  11.3 us
  transfers between devices with their start and end apart: 2, of which 2 were waited for; matrix products, arithmetic and copies ran while one was open for 0% of the time, Pallas kernels for 0%

commit v1 on v0

--- a/solution.py
+++ b/solution.py
@@ -2,6 +2,30 @@
 import jax.numpy as jnp
 from jax import lax
 from jax.sharding import PartitionSpec as P
+
+
+def in_blocks(x, dim, length):
+    shape = x.shape
+    blocks = x.reshape(*shape[:dim], length, shape[dim] // length, *shape[dim + 1 :])
+    return jnp.moveaxis(blocks, dim, 0)
+
+
+def in_order(tiles, dim):
+    lengths = list(tiles.shape[1:])
+    lengths[dim] *= tiles.shape[0]
+    return jnp.moveaxis(tiles, 0, dim).reshape(lengths)
+
+
+def rotated_exchange(x, axis, split_dim, concat_dim):
+    peers, index = (lax.axis_size(axis), lax.axis_index(axis))
+    parts = in_blocks(x, split_dim, peers)
+    out = parts
+    for step in range(1, peers):
+        target, source = ((index + step) % peers, (index - step) % peers)
+        sent = lax.dynamic_index_in_dim(parts, target, 0)
+        other = lax.ppermute(sent, axis, [(i, (i + step) % peers) for i in range(peers)])
+        out = lax.dynamic_update_slice_in_dim(out, other, source, axis=0)
+    return in_order(out, concat_dim)
 
 
 def polynomial(coef_row, values):
@@ -48,11 +72,7 @@
     active_flag = active_mask[0, 0].astype(jnp.float32)
     layer = march_brick(volume[0, 0], transfer_coef, active_flag, density_scale)
     slab_ranks = lax.dynamic_slice_in_dim(member_order, lax.axis_index("grp"), 1, 0)[0]
-    slab_image = over_tree(
-        reorder(
-            lax.all_to_all(layer[None], "mem", split_axis=2, concat_axis=0, tiled=True), slab_ranks
-        )
-    )
+    slab_image = over_tree(reorder(rotated_exchange(layer[None], "mem", 2, 0), slab_ranks))
     return over_tree(
         reorder(
             lax.all_to_all(slab_image[None], "grp", split_axis=3, concat_axis=0, tiled=True),

time: 450 us -> 277 us (0.62)
  other arithmetic: 285 us -> 143 us
  waiting for transfers between devices: 118 us -> 65.7 us
  starting transfers between devices: 10.6 us -> 25.3 us
  local copies, waits for them, and re-layouts: 34.6 us -> 40.5 us
    concatenate x2 -> x1, other arithmetic: 117 us -> 11.8 us  [march_brick(): return jnp.concatenate([colour, coverage[None]], 0) * active_flag]
    all_to_all x1 -> x0, waiting for transfers between devices: 92.2 us -> none  [body(): lax.all_to_all(layer[None], 'mem', split_axis=2, concat_axis=0, tiled=True)]
    add x4, other arithmetic: 125 us -> 51.1 us  [polynomial(): coef_row[0]]
    ppermute x0 -> x7, waiting for transfers between devices: none -> 38.8 us  [rotated_exchange(): lax.ppermute(sent, axis, [(i, (i + step) % peers) for i in range(peers)])]
    reshape x0 -> x1, other arithmetic: none -> 24.5 us  [in_order(): return jnp.moveaxis(tiles, 0, dim).reshape(lengths)]
    ppermute x0 -> x7, starting transfers between devices: none -> 20.4 us  [rotated_exchange(): lax.ppermute(sent, axis, [(i, (i + step) % peers) for i in range(peers)])]
    mul x1, other arithmetic: 7.07 us -> 21.7 us  [march_brick(): return jnp.concatenate([colour, coverage[None]], 0) * active_flag]
    dynamic_update_slice x0 -> x7, local copies, waits for them, and re-layouts: none -> 13.8 us  [rotated_exchange(): out = lax.dynamic_update_slice_in_dim(out, other, source, axis=0)]
  transfers between devices with their start and end apart: 2 -> 8, of which waited for: 2 -> 2; matrix products, arithmetic and copies ran while one was open for 0% -> 14% of each run, Pallas kernels for 0% -> 0%
where the time goes in v1:
time: 277 us; the launch traced here: 276 us
  other arithmetic  143 us (52%)
  waiting for transfers between devices  65.7 us (24%)
  local copies, waits for them, and re-layouts  40.5 us (15%)
  starting transfers between devices  25.3 us (9%)
    add x4, other arithmetic, polynomial(): coef_row[0]  51.1 us
    ppermute x7, waiting for transfers between devices, rotated_exchange(): lax.ppermute(sent, axis, [(i, (i + step) % peers) for i in range(peers)])  38.8 us
    all_to_all x1, waiting for transfers between devices, body(): lax.all_to_all(slab_image[None], 'grp', split_axis=3, concat_axis=0, tile...  26.9 us
    reshape x1, other arithmetic, in_order(): return jnp.moveaxis(tiles, 0, dim).reshape(lengths)  24.5 us
    mul x3, other arithmetic, march_brick(): colour = colour + (jnp.exp(-optical_depth) * opacity)[None] * tinted  22.2 us
    mul x1, other arithmetic, march_brick(): return jnp.concatenate([colour, coverage[None]], 0) * active_flag  21.7 us
    ppermute x7, starting transfers between devices, rotated_exchange(): lax.ppermute(sent, axis, [(i, (i + step) % peers) for i in range(peers)])  20.4 us
    dynamic_update_slice x7, local copies, waits for them, and re-layouts, rotated_exchange(): out = lax.dynamic_update_slice_in_dim(out, other, source, axis=0)  13.8 us
  transfers between devices with their start and end apart: 8, of which 2 were waited for; matrix products, arithmetic and copies ran while one was open for 14% of the time, Pallas kernels for 0%

profile of v1, /device:TPU:2, one launch (start us, length us, event | category | flops | bytes accessed | tf_op | source)
XLA Modules:
  0.0 275.6 jit_solution(9909815992452212457)
XLA Ops:
  0.7 6.7 %fusion.62 = (f32[1,1,1,512,1024]{4,3,2,1,0:T(8,128)S(1)}, f32[1,1,1,512,1024]{4,3,2,1,0:T(8,128)S(1)}, f32[1,1,1,512,1024]{4,3,2,1,0:T(8,128)S(1)}, f32[1,1,1,5...) fusion(f32[1,1,8,512,1024]{4,3,2,1,0:T(8,128)} %param.5), kind=kLoop, calls=%fused_computation.150 | loop fusion | bytes 33554432 | tf_op jit(solution)/shard_map/slice | solution.py:39
  8.4 12.8 %multiply_add_fusion.4 = (f32[1,8,64,1024]{3,2,1,0:T(8,128)}, f32[1,8,64,1024]{3,2,1,0:T(8,128)}, f32[1,8,64,1024]{3,2,1,0:T(8,128)}, f32[1,8,64,1024]{3,2,1,0:T...) fusion(f32[1,8,64,1024]{3,2,1,0:T(8,128)S(1)} %bitcast.118, f32[]{:T(128)} %bitcast.10, f32[]{:T(128)} %bitcast.9, ...), kind=kLoop, calls=%fused_computation.60 | loop fusion | flops 18874368 | bytes 16777264 | tf_op jit(solution)/shard_map/add | solution.py:32
  21.3 12.8 %multiply_add_fusion.10 = (f32[1,8,64,1024]{3,2,1,0:T(8,128)}, f32[1,8,64,1024]{3,2,1,0:T(8,128)}, f32[1,8,64,1024]{3,2,1,0:T(8,128)}, f32[1,8,64,1024]{3,2,1,0:...) fusion(f32[1,8,64,1024]{3,2,1,0:T(8,128)S(1)} %bitcast.105, f32[]{:T(128)} %bitcast.10, f32[]{:T(128)} %bitcast.9, ...), kind=kLoop, calls=%fused_computation.69 | loop fusion | flops 18874368 | bytes 16777264 | tf_op jit(solution)/shard_map/add | solution.py:32
  34.1 12.8 %multiply_add_fusion.16 = (f32[1,8,64,1024]{3,2,1,0:T(8,128)}, f32[1,8,64,1024]{3,2,1,0:T(8,128)}, f32[1,8,64,1024]{3,2,1,0:T(8,128)}, f32[1,8,64,1024]{3,2,1,0:...) fusion(f32[1,8,64,1024]{3,2,1,0:T(8,128)S(1)} %bitcast.101, f32[]{:T(128)} %bitcast.10, f32[]{:T(128)} %bitcast.9, ...), kind=kLoop, calls=%fused_computation.79 | loop fusion | flops 18874368 | bytes 16777264 | tf_op jit(solution)/shard_map/add | solution.py:32
  46.9 12.7 %multiply_add_fusion.22 = (f32[1,8,64,1024]{3,2,1,0:T(8,128)}, f32[1,8,64,1024]{3,2,1,0:T(8,128)}, f32[1,8,64,1024]{3,2,1,0:T(8,128)}, f32[1,8,64,1024]{3,2,1,0:...) fusion(f32[1,8,64,1024]{3,2,1,0:T(8,128)S(1)} %bitcast.115, f32[]{:T(128)} %bitcast.10, f32[]{:T(128)} %bitcast.9, ...), kind=kLoop, calls=%fused_computation.89 | loop fusion | flops 18874368 | bytes 16777264 | tf_op jit(solution)/shard_map/add | solution.py:32
  59.6 11.8 %fusion.42 = f32[1,1,8,64,1024]{4,3,1,2,0:T(8,128)} fusion(f32[1,8,64,1024]{3,2,1,0:T(8,128)} %bitcast.119, f32[1,8,64,1024]{3,2,1,0:T(8,128)} %bitcast.122, f32[1,8,64,1024]{3,2,1,0:T(8,128)} %bitcast.106, f32[1,8,64,1024]{3,2,1,0:T(8,128)} %bitcast.125, f32[1,8,64,1024]{3,2,1,0:T(8,128)S(1)} %bitcast.102, f32[1,8,64,1024]{3,2,1,0:T(8,128)} %bitcast.113, ...), kind=kLoop, calls=%fused_computation.56 | loop fusion | flops 34603008 | bytes 18874384 | tf_op jit(solution)/shard_map/concatenate | solution.py:48
  71.4 8.5 %subtract_multiply_fusion.4 = (f32[8,64,1024]{2,1,0:T(8,128)}, f32[8,64,1024]{2,1,0:T(8,128)S(1)}, f32[8,64,1024]{2,1,0:T(8,128)}, f32[8,64,1024]{2,1,0:T(8,128)}, f32[8,64,1024]{2,1,0:T(8,128)}) fusion(f32[8,64,1024]{2,1,0:T(8,128)S(1)} %bitcast.103, f32[]{:T(128)} %bitcast.5, f32[]{:T(128)} %bitcast.4, f32[]{:T(128)} %bitcast.3, f32[]{:T(128)} %bitcast.1, ...), kind=kLoop, calls=%fused_computation.80 | loop fusion | flops 24641536 | bytes 18874384 | tf_op jit(solution)/shard_map/mul | solution.py:45
  80.0 7.1 %subtract_multiply_fusion.2 = (f32[8,64,1024]{2,1,0:T(8,128)}, f32[8,64,1024]{2,1,0:T(8,128)S(1)}, f32[8,64,1024]{2,1,0:T(8,128)}) fusion(f32[8,64,1024]{2,1,0:T(8,128)S(1)} %bitcast.107, f32[]{:T(128)} %bitcast.5, f32[]{:T(128)} %bitcast.4, f32[]{:T(128)} %bitcast.3, f32[]{:T(128)} %bitcast.1, f32[8,64,1024]{2,1,0:T(8,128)S(1)} %bitcast.126, ...), kind=kLoop, calls=%fused_computation.70 | loop fusion | flops 17825792 | bytes 14680080 | tf_op jit(solution)/shard_map/mul | solution.py:45
  87.0 6.6 %subtract_multiply_fusion.1 = (f32[8,64,1024]{2,1,0:T(8,128)}, f32[8,64,1024]{2,1,0:T(8,128)}) fusion(f32[8,64,1024]{2,1,0:T(8,128)S(1)} %bitcast.123, f32[]{:T(128)} %bitcast.5, f32[]{:T(128)} %bitcast.4, f32[]{:T(128)} %bitcast.3, f32[]{:T(128)} %bitcast.1, f32[8,64,1024]{2,1,0:T(8,128)S(1)} %get-tuple-element.8, f32[8,64,1024]{2,1,0:T(8,128)S(1)} %bitcast.108, ...), kind=kLoop, calls=%fused_computation.65 | loop fusion | flops 17825792 | bytes 12582928 | tf_op jit(solution)/shard_map/mul | solution.py:45
  93.7 21.7 %maximum_multiply_fusion = f32[1,4,8,64,1024]{4,3,1,2,0:T(8,128)S(1)} fusion(f32[1,1,8,64,1024]{4,3,1,2,0:T(8,128)} %fusion.42, f32[]{:T(128)} %bitcast.35, f32[1,8,64,1024]{3,2,1,0:T(8,128)} %get-tuple-element.52, f32[1,8,64,1024]{3,2,1,0:T(8,128)} %get-tuple-element.53, f32[1,8,64,1024]{3,2,1,0:T(8,128)S(1)} %copy-done.15, ...), kind=kLoop, calls=%fused_computation.2 | loop fusion | flops 90701824 | bytes 77594624 | tf_op jit(solution)/shard_map/mul | solution.py:48
  115.3 3.1 %dynamic-slice_bitcast_fusion = (f32[1,1,4,64,1024]{4,3,2,1,0:T(8,128)}, f32[1,1,4,64,1024]{4,3,2,1,0:T(8,128)}, f32[1,1,4,64,1024]{4,3,2,1,0:T(8,128)}, f32[1,1...) fusion(f32[1,4,8,64,1024]{4,3,1,2,0:T(8,128)S(1)} %maximum_mult, ...), kind=kLoop, calls=%fused_computation.114 | loop fusion | bytes 14680092 | tf_op jit(solution)/shard_map/jit(dynamic_index_in_dim)/dynamic_slice | solution.py:25
  118.4 1.5 collective-permute-start.1
  119.9 1.2 collective-permute-start.2
  121.1 1.7 collective-permute-start.3
  122.8 24.5 %fusion.64 = f32[8,4,64,1024]{3,2,1,0:T(8,128)} fusion(f32[]{:T(128)} %bitcast.35, f32[1,1,8,64,1024]{4,3,1,2,0:T(8,128)} %fusion.42, f32[1,8,64,1024]{3,2,1,0:T(8,128)} %get-tuple-element.52, f32[1,8,64,1024]{3,2,1,0:T(8,128)} %get-tuple-element.53, f32[1,8,64,1024]{3,2,1,0:T(8,128)S(1)} %copy-done.15, f32[1,8,64,1024]{3,2,1,0:T(8,128)} %get-tuple-element.71, ...), kind=kLoop, calls=%fused_computation.152 | loop fusion | flops 90701824 | bytes 77594624 | tf_op jit(solution)/shard_map/reshape | solution.py:16
  148.3 2.3 bitcast_dynamic-update-slice_fusion.6
  150.6 15.4 %collective-permute-start.6 = (f32[1,1,4,64,1024]{4,3,2,1,0:T(8,128)S(1)}, f32[1,1,4,64,1024]{4,3,2,1,0:T(8,128)S(1)}, u32[]{:S(2)}, u32[]{:S(2)}) collective-permute-start(f32[1,1,4,64,1024]{4,3,2,1,0:T(8,128)S(1)} %copy-done.16), channel_id=1, source_target_pairs={{0,7},{1,0},{2,1},{3,2},{4,3},{5,4},{6,5},{7,6},{8,15},{9,8},{10,9... | collective-permute-start | bytes 3145736 | tf_op jit(solution)/shard_map/ppermute | solution.py:26
  166.0 2.3 bitcast_dynamic-update-slice_fusion.5
  168.3 2.4 bitcast_dynamic-update-slice_fusion.4
  170.7 2.3 bitcast_dynamic-update-slice_fusion.3
  173.0 38.8 %collective-permute-done.4 = f32[1,1,4,64,1024]{4,3,2,1,0:T(8,128)} collective-permute-done((f32[1,1,4,64,1024]{4,3,2,1,0:T(8,128)}, f32[1,1,4,64,1024]{4,3,2,1,0:T(8,128)}, u32[]{:S(2)}, u32[]{:S(2)}) %collective-permute-start.4) | collective-permute-done | bytes 1048608 | tf_op jit(solution)/shard_map/ppermute | solution.py:26
  211.8 2.3 bitcast_dynamic-update-slice_fusion.2
  214.1 1.1 bitcast_dynamic-update-slice_fusion.1
  216.3 7.7 %gather_fusion = f32[8,4,64,1024]{3,2,1,0:T(8,128)} fusion(f32[8,4,64,1024]{3,2,1,0:T(8,128)} %bitcast_dynamic-update-slice_fusion, s32[1024]{0:T(1024)S(1)} %pad_clamp_fusion.1), kind=kCustom, calls=%fused_computation | custom fusion | bytes 16777248 | tf_op jit(solution)/shard_map/jit(_take)/gather | solution.py:57
  224.0 4.4 %broadcast_select_fusion = f32[8,4,64,1024]{3,2,1,0:T(8,128)S(1)} fusion(f32[8,4,64,1024]{3,2,1,0:T(8,128)} %gather_fusion, pred[8]{0:T(512)(128)(4,1)S(1)} %compare_and_fusion), kind=kLoop, calls=%fused_computation.52 | loop fusion | flops 2097152 | bytes 16777224 | tf_op jit(solution)/shard_map/jit(_take)/select_n | solution.py:57
  229.1 1.1 multiply_add_fusion
  231.4 1.1 copy.14
  232.5 2.9 %reshape.2203 = f32[4,1,65536]{2,1,0:T(1,128)} reshape(f32[1024,1,4,64]{3,2,1,0:T(4,128)S(1)} %bitcast.127) | data formatting | bytes 2097152
  235.5 4.9 %all-to-all-start = ((f32[4,1,65536]{2,1,0:T(1,128)}), f32[4,1,65536]{2,1,0:T(1,128)S(1)}, u32[]{:S(2)}, u32[]{:S(2)}) async-start(f32[4,1,65536]{2,1,0:T(1,128)} %reshape.2203), calls=%async_computation | async-start | bytes 2097152 | tf_op jit(solution)/shard_map/all_to_all | solution.py:78
  240.4 26.9 %all-to-all-done = f32[4,1,65536]{2,1,0:T(1,128)S(1)} async-done(((f32[4,1,65536]{2,1,0:T(1,128)}), f32[4,1,65536]{2,1,0:T(1,128)S(1)}, u32[]{:S(2)}, u32[]{:S(2)}) %all-to-all-start) | async-done | bytes 1048608 | tf_op jit(solution)/shard_map/all_to_all | solution.py:78
  267.8 3.8 %reduce = f32[4,65536]{1,0:T(4,128)S(1)} reduce(f32[4,1,65536]{2,1,0:T(1,128)S(1)} %all-to-all-done, f32[]{:T(128)} %broadcast.2377), dimensions={1}, to_apply=%all_to_all.13.reduce_sub_computation | reduce | bytes 2097156 | tf_op jit(solution)/shard_map/all_to_all | solution.py:78
  271.6 1.4 reshape.2204
  (74 shorter events, 7.7 us)
Async XLA Ops:
  0.0 147.5 %copy-start = (s32[4,8]{1,0:T(4,128)S(1)}, s32[4,8]{1,0:T(4,128)}, u32[]{:S(2)}) copy-start(s32[4,8]{1,0:T(4,128)} %param.8) | copy-start | bytes 388
  0.7 6.7 %copy-start.17 = (f32[4,4]{1,0:T(4,128)S(1)}, f32[4,4]{1,0:T(4,128)}, u32[]{:S(2)}) copy-start(f32[4,4]{1,0:T(4,128)} %param.6) | copy-start | bytes 196
  7.4 13.9 %copy-start.9 = (f32[1,1,1,512,1024]{4,3,2,1,0:T(8,128)}, f32[1,1,1,512,1024]{4,3,2,1,0:T(8,128)S(1)}, u32[]{:S(2)}) copy-start(f32[1,1,1,512,1024]{4,3,2,1,0:T(8,128)S(1)} %get-tuple-element.15) | copy-start | bytes 6291460
  7.4 13.9 %copy-start.11 = (f32[1,1,1,512,1024]{4,3,2,1,0:T(8,128)}, f32[1,1,1,512,1024]{4,3,2,1,0:T(8,128)S(1)}, u32[]{:S(2)}) copy-start(f32[1,1,1,512,1024]{4,3,2,1,0:T(8,128)S(1)} %get-tuple-element.16) | copy-start | bytes 6291460
  7.4 13.9 %copy-start.1 = (f32[1,1,1,512,1024]{4,3,2,1,0:T(8,128)}, f32[1,1,1,512,1024]{4,3,2,1,0:T(8,128)S(1)}, u32[]{:S(2)}) copy-start(f32[1,1,1,512,1024]{4,3,2,1,0:T(8,128)S(1)} %get-tuple-element.10) | copy-start | bytes 6291460
  7.4 13.9 %copy-start.13 = (f32[1,1,1,512,1024]{4,3,2,1,0:T(8,128)}, f32[1,1,1,512,1024]{4,3,2,1,0:T(8,128)S(1)}, u32[]{:S(2)}) copy-start(f32[1,1,1,512,1024]{4,3,2,1,0:T(8,128)S(1)} %get-tuple-element.11) | copy-start | bytes 6291460
  7.4 26.6 %copy-start.5 = (f32[1,1,1,512,1024]{4,3,2,1,0:T(8,128)}, f32[1,1,1,512,1024]{4,3,2,1,0:T(8,128)S(1)}, u32[]{:S(2)}) copy-start(f32[1,1,1,512,1024]{4,3,2,1,0:T(8,128)S(1)} %get-tuple-element.13) | copy-start | bytes 6291460
  7.5 39.4 %copy-start.3 = (f32[1,1,1,512,1024]{4,3,2,1,0:T(8,128)}, f32[1,1,1,512,1024]{4,3,2,1,0:T(8,128)S(1)}, u32[]{:S(2)}) copy-start(f32[1,1,1,512,1024]{4,3,2,1,0:T(8,128)S(1)} %get-tuple-element.9) | copy-start | bytes 6291460
  7.5 39.4 %copy-start.7 = (f32[1,1,1,512,1024]{4,3,2,1,0:T(8,128)}, f32[1,1,1,512,1024]{4,3,2,1,0:T(8,128)S(1)}, u32[]{:S(2)}) copy-start(f32[1,1,1,512,1024]{4,3,2,1,0:T(8,128)S(1)} %get-tuple-element.14) | copy-start | bytes 6291460
  59.6 11.8 %copy-start.4 = (f32[1,1,1,512,1024]{4,3,2,1,0:T(8,128)S(1)}, f32[1,1,1,512,1024]{4,3,2,1,0:T(8,128)}, u32[]{:S(2)}) copy-start(f32[1,1,1,512,1024]{4,3,2,1,0:T(8,128)} %copy-done.3) | copy-start | bytes 6291460
  59.6 11.8 %copy-start.6 = (f32[1,1,1,512,1024]{4,3,2,1,0:T(8,128)S(1)}, f32[1,1,1,512,1024]{4,3,2,1,0:T(8,128)}, u32[]{:S(2)}) copy-start(f32[1,1,1,512,1024]{4,3,2,1,0:T(8,128)} %copy-done.5) | copy-start | bytes 6291460
  59.6 11.8 %copy-start.8 = (f32[1,1,1,512,1024]{4,3,2,1,0:T(8,128)S(1)}, f32[1,1,1,512,1024]{4,3,2,1,0:T(8,128)}, u32[]{:S(2)}) copy-start(f32[1,1,1,512,1024]{4,3,2,1,0:T(8,128)} %copy-done.7) | copy-start | bytes 6291460
  71.4 8.5 %copy-start.2 = (f32[1,1,1,512,1024]{4,3,2,1,0:T(8,128)S(1)}, f32[1,1,1,512,1024]{4,3,2,1,0:T(8,128)}, u32[]{:S(2)}) copy-start(f32[1,1,1,512,1024]{4,3,2,1,0:T(8,128)} %copy-done.1) | copy-start | bytes 6291460
  71.4 8.5 %copy-start.14 = (f32[1,1,1,512,1024]{4,3,2,1,0:T(8,128)S(1)}, f32[1,1,1,512,1024]{4,3,2,1,0:T(8,128)}, u32[]{:S(2)}) copy-start(f32[1,1,1,512,1024]{4,3,2,1,0:T(8,128)} %copy-done.13) | copy-start | bytes 6291460
  79.9 7.1 %copy-start.10 = (f32[1,1,1,512,1024]{4,3,2,1,0:T(8,128)S(1)}, f32[1,1,1,512,1024]{4,3,2,1,0:T(8,128)}, u32[]{:S(2)}) copy-start(f32[1,1,1,512,1024]{4,3,2,1,0:T(8,128)} %copy-done.9) | copy-start | bytes 6291460
  79.9 7.1 %copy-start.12 = (f32[1,1,1,512,1024]{4,3,2,1,0:T(8,128)S(1)}, f32[1,1,1,512,1024]{4,3,2,1,0:T(8,128)}, u32[]{:S(2)}) copy-start(f32[1,1,1,512,1024]{4,3,2,1,0:T(8,128)} %copy-done.11) | copy-start | bytes 6291460
  87.0 6.6 %copy-start.15 = (f32[1,8,64,1024]{3,2,1,0:T(8,128)S(1)}, f32[1,8,64,1024]{3,2,1,0:T(8,128)}, u32[]{:S(2)}) copy-start(f32[1,8,64,1024]{3,2,1,0:T(8,128)} %get-tuple-element.51) | copy-start | bytes 6291460
  118.4 29.3 %collective-permute-start = (f32[1,1,4,64,1024]{4,3,2,1,0:T(8,128)}, f32[1,1,4,64,1024]{4,3,2,1,0:T(8,128)}, u32[]{:S(2)}, u32[]{:S(2)}) collective-permute-start(f32[1,1,4,64,1024]{4,3,2,1,0:T(8,128)} %get-tuple-element.23), channel_id=1, source_target_pairs={{0,1},{1,2},{2,3},{3,4},{4,5},{5,6},{6,7},{7,0},{8,9},{9,10},{10,1... | collective-permute-start | bytes 3145736 | tf_op jit(solution)/shard_map/ppermute | solution.py:26
  118.4 32.2 %collective-permute-start.1 = (f32[1,1,4,64,1024]{4,3,2,1,0:T(8,128)}, f32[1,1,4,64,1024]{4,3,2,1,0:T(8,128)}, u32[]{:S(2)}, u32[]{:S(2)}) collective-permute-start(f32[1,1,4,64,1024]{4,3,2,1,0:T(8,128)} %get-tuple-element.22), channel_id=1, source_target_pairs={{0,2},{1,3},{2,4},{3,5},{4,6},{5,7},{6,0},{7,1},{8,10},{9,11},{10,... | collective-permute-start | bytes 3145736 | tf_op jit(solution)/shard_map/ppermute | solution.py:26
  119.9 48.4 %collective-permute-start.2 = (f32[1,1,4,64,1024]{4,3,2,1,0:T(8,128)}, f32[1,1,4,64,1024]{4,3,2,1,0:T(8,128)}, u32[]{:S(2)}, u32[]{:S(2)}) collective-permute-start(f32[1,1,4,64,1024]{4,3,2,1,0:T(8,128)} %get-tuple-element.21), channel_id=1, source_target_pairs={{0,3},{1,4},{2,5},{3,6},{4,7},{5,0},{6,1},{7,2},{8,11},{9,12},{10,... | collective-permute-start | bytes 3145736 | tf_op jit(solution)/shard_map/ppermute | solution.py:26
  121.1 49.6 %collective-permute-start.3 = (f32[1,1,4,64,1024]{4,3,2,1,0:T(8,128)}, f32[1,1,4,64,1024]{4,3,2,1,0:T(8,128)}, u32[]{:S(2)}, u32[]{:S(2)}) collective-permute-start(f32[1,1,4,64,1024]{4,3,2,1,0:T(8,128)} %get-tuple-element.20), channel_id=1, source_target_pairs={{0,4},{1,5},{2,6},{3,7},{4,0},{5,1},{6,2},{7,3},{8,12},{9,13},{10,... | collective-permute-start | bytes 3145736 | tf_op jit(solution)/shard_map/ppermute | solution.py:26
  122.8 89.0 %collective-permute-start.4 = (f32[1,1,4,64,1024]{4,3,2,1,0:T(8,128)}, f32[1,1,4,64,1024]{4,3,2,1,0:T(8,128)}, u32[]{:S(2)}, u32[]{:S(2)}) collective-permute-start(f32[1,1,4,64,1024]{4,3,2,1,0:T(8,128)} %get-tuple-element.19), channel_id=1, source_target_pairs={{0,5},{1,6},{2,7},{3,0},{4,1},{5,2},{6,3},{7,4},{8,13},{9,14},{10,... | collective-permute-start | bytes 3145736 | tf_op jit(solution)/shard_map/ppermute | solution.py:26
  147.4 3.2 %copy-start.16 = (f32[1,1,4,64,1024]{4,3,2,1,0:T(8,128)S(1)}, f32[1,1,4,64,1024]{4,3,2,1,0:T(8,128)}, u32[]{:S(2)}) copy-start(f32[1,1,4,64,1024]{4,3,2,1,0:T(8,128)} %get-tuple-element.17) | copy-start | bytes 3145732
  147.7 66.5 %collective-permute-start.5 = (f32[1,1,4,64,1024]{4,3,2,1,0:T(8,128)}, f32[1,1,4,64,1024]{4,3,2,1,0:T(8,128)S(1)}, u32[]{:S(2)}, u32[]{:S(2)}) collective-permute-start(f32[1,1,4,64,1024]{4,3,2,1,0:T(8,128)} %get-tuple-element.18), channel_id=1, source_target_pairs={{0,6},{1,7},{2,0},{3,1},{4,2},{5,3},{6,4},{7,5},{8,14},{9,15},{10,... | collective-permute-start | bytes 3145736 | tf_op jit(solution)/shard_map/ppermute | solution.py:26
  150.6 64.6 %collective-permute-start.6 = (f32[1,1,4,64,1024]{4,3,2,1,0:T(8,128)S(1)}, f32[1,1,4,64,1024]{4,3,2,1,0:T(8,128)S(1)}, u32[]{:S(2)}, u32[]{:S(2)}) collective-permute-start(f32[1,1,4,64,1024]{4,3,2,1,0:T(8,128)S(1)} %copy-done.16), channel_id=1, source_target_pairs={{0,7},{1,0},{2,1},{3,2},{4,3},{5,4},{6,5},{7,6},{8,15},{9,8},{10,9... | collective-permute-start | bytes 3145736 | tf_op jit(solution)/shard_map/ppermute | solution.py:26
  232.5 7.8 %copy-start.18 = (s32[4]{0:T(128)S(1)}, s32[4]{0:T(128)}, u32[]{:S(2)}) copy-start(s32[4]{0:T(128)} %param.7) | copy-start | bytes 52
  235.5 31.9 %all-to-all-start = ((f32[4,1,65536]{2,1,0:T(1,128)}), f32[4,1,65536]{2,1,0:T(1,128)S(1)}, u32[]{:S(2)}, u32[]{:S(2)}) async-start(f32[4,1,65536]{2,1,0:T(1,128)} %reshape.2203), calls=%async_computation | async-start | bytes 2097152 | tf_op jit(solution)/shard_map/all_to_all | solution.py:78
